TPU v7x, 256 devices: a whole 4x4x8 slice. The times are simulated.
256 devices in a mesh: section: 16 (over z, core), mp: 8 (over x, y_hi), dp: 2 (over y_lo).
Axes of the slice: x: 4, y: 4 (y_hi: 2, y_lo: 2; y = y_hi * 2 + y_lo), z: 8, core: 2. Of those that a mesh axis runs over, the one named last changes fastest.
Arguments:
- enc_out: bfloat16 [2, 512, 4096], P('dp', 'mp', 'section'), may hold values from -6 to 6
- kv_weight: bfloat16 [16, 4096, 2, 4096], P('section', None, None, 'mp'), may hold values from -0.09375 to 0.09375
- dec_query: bfloat16 [16, 2, 512, 4096], P('section', 'dp', None, 'mp'), may hold values from -120 to 120
- ctx_grad: bfloat16 [16, 2, 512, 4096], P('section', 'dp', None, 'mp'), may hold values from -6 to 6
- enc_seg: int32 [2, 512], P('dp'), may hold values from 0 to 7, never falling along the last dimension, each value on 1 to 128 neighbouring positions
- dec_seg: int32 [2, 512], P('dp'), may hold values from 0 to 7, never falling along the last dimension, each value on 1 to 128 neighbouring positions
Outputs:
- context: bfloat16 [16, 2, 512, 4096], P('section', 'dp', None, 'mp')
- enc_grad: float32 [2, 512, 4096], P('dp', 'mp', 'section')
Inputs may be any that keep to these rules, and one draw needn't show every extreme that they name: `enc_seg`: document ids never fall along a sequence and every id appears. `dec_seg`: document ids never fall along a sequence and every id appears.
All inputs are finite; a program needn't handle non-finite values.
Results may differ from a plain program's by a relative error of at most 0.04.
The roundings to bfloat16 on the way count: a program that leaves them out, or rounds other values in their place, can miss the bound.
Values may be sent and summed in bfloat16 or wider, within the bound.
No kernel may reach another device: no remote copies, remote signals or barrier semaphores. Data moves between devices by JAX's collectives and lax.ppermute only.
A program may use at most 128 MiB of HBM per device.

v0:
```python
import jax
import jax.numpy as jnp
from jax import lax
from jax.sharding import PartitionSpec as P

HD = 256


def attend(query, keys, values, grad, same_doc):
    scale = HD ** (-0.5)
    scores = jnp.einsum("qhd,khd->hqk", query, keys, preferred_element_type=jnp.float32) * scale
    scores = jnp.where(same_doc[None], scores, -1e30)
    top_score = jnp.max(scores, axis=-1, keepdims=True)
    raised = jnp.exp(scores - top_score)
    probs = raised / jnp.sum(raised, axis=-1, keepdims=True)
    probs_low = probs.astype(jnp.bfloat16)
    context = jnp.einsum(
        "hqk,khd->qhd", probs_low, values, preferred_element_type=jnp.float32
    ).astype(jnp.bfloat16)
    grad_values = jnp.einsum(
        "hqk,qhd->khd", probs_low, grad, preferred_element_type=jnp.float32
    ).astype(jnp.bfloat16)
    grad_probs = jnp.einsum("qhd,khd->hqk", grad, values, preferred_element_type=jnp.float32)
    inner_sum = jnp.sum(probs * grad_probs, axis=-1, keepdims=True)
    grad_scores = (probs * (grad_probs - inner_sum) * scale).astype(jnp.bfloat16)
    grad_keys = jnp.einsum(
        "hqk,qhd->khd", grad_scores, query, preferred_element_type=jnp.float32
    ).astype(jnp.bfloat16)
    return (context, grad_keys, grad_values)


def per_device(enc_out, kv_weight, dec_query, ctx_grad, enc_seg, dec_seg):
    shard_rows = enc_out[0]
    width = kv_weight.shape[3]
    model_width = kv_weight.shape[1]
    flat_weight = kv_weight[0].reshape(model_width, 2 * width)
    all_tokens = lax.all_gather(shard_rows, "mp", axis=0, tiled=True)
    weight_rows = flat_weight
    key_values = jnp.dot(
        lax.all_gather(all_tokens, "section", axis=1, tiled=True),
        weight_rows,
        preferred_element_type=jnp.float32,
    ).astype(jnp.bfloat16)
    length = key_values.shape[0]
    heads_here = width // HD
    decoder = dec_query.shape[2]
    keys = key_values[:, :width].reshape(length, heads_here, HD)
    values = key_values[:, width:].reshape(length, heads_here, HD)
    same_doc = dec_seg[0][:, None] == enc_seg[0][None, :]
    query = dec_query[0, 0].reshape(decoder, heads_here, HD)
    grad = ctx_grad[0, 0].reshape(decoder, heads_here, HD)
    context, grad_keys, grad_values = attend(query, keys, values, grad, same_doc)
    grad_both = jnp.concatenate(
        [grad_keys.reshape(length, width), grad_values.reshape(length, width)], axis=1
    )
    weight_rows = flat_weight
    feature_share = lax.psum_scatter(
        lax.dot_general(
            weight_rows, grad_both, (((1,), (1,)), ((), ())), preferred_element_type=jnp.float32
        ).astype(jnp.bfloat16),
        "section",
        scatter_dimension=0,
        tiled=True,
    )
    owned_grad = (
        lax.psum_scatter(feature_share, "mp", scatter_dimension=1, tiled=True).astype(jnp.float32).T
    )
    return (context.reshape(1, 1, decoder, width), owned_grad[None])


def solution(mesh):
    placed = (
        P("dp", "mp", "section"),
        P("section", None, None, "mp"),
        P("section", "dp", None, "mp"),
        P("section", "dp", None, "mp"),
        P("dp", None),
        P("dp", None),
    )
    return jax.shard_map(
        per_device,
        mesh=mesh,
        in_specs=placed,
        out_specs=(P("section", "dp", None, "mp"), P("dp", "mp", "section")),
        check_vma=False,
    )
```

profile of v0, /device:TPU:2, one launch (start us, length us, event | category | flops | bytes accessed | tf_op | source)
XLA Modules:
  0.0 273.9 jit_solution(1828879622895667745)
XLA Ops:
  7.2 0.0 all-gather.4.cloned.1.call-start
  7.2 36.3 %all-gather = bf16[1,512,256]{2,1,0:T(8,128)(2,1)} all-gather(bf16[1,64,256]{2,1,0:T(8,128)(2,1)} %param.6), channel_id=2, replica_groups=mesh['section'=16,'mp'=8,'dp'=2] {'mp'}, dimensions={1}, use_global_device_ids=true | all-gather | bytes 294912 | tf_op jit(solution)/shard_map/all_gather | solution.py:37
  43.5 0.0 all-gather.4.cloned.1.call-update
  43.5 0.0 reduce-scatter.3.cloned.1.call-start
  43.6 2.1 copy.23
  45.7 1.3 copy.24
  46.9 9.5 %copy.27 = bf16[512,8,2,512]{3,1,2,0:T(8,128)(2,1)} copy(bf16[512,8,2,512]{3,2,1,0:T(2,128)(2,1)} %bitcast.75) | data formatting | bytes 16777216
  56.4 0.2 broadcast_compare_fusion
  56.6 38.7 %all-gather.4.cloned.1.call-done = bf16[1,512,4096]{2,1,0:T(8,128)(2,1)} async-done(((bf16[1,512,256]{2,1,0:T(8,128)(2,1)}), bf16[1,512,4096]{2,1,0:T(8,128)(2,1)}) %all-gather.4.cloned.1.call-update) | async-done | bytes 4194320 | tf_op jit(solution)/shard_map/all_gather | solution.py:40
  95.3 9.1 %fusion.10 = bf16[512,1024]{1,0:T(8,128)(2,1)S(1)} fusion(bf16[4096,1024]{1,0:T(8,128)(2,1)} %bitcast.76, bf16[1,512,4096]{2,1,0:T(8,128)(2,1)} %all-gather.4.cloned.1.call-done), kind=kOutput, calls=%fused_computation.15 | convolution fusion | flops 4295491584 | bytes 13631488 | tf_op jit(solution)/shard_map/dot_general | solution.py:39
  104.5 0.9 fusion.43
  105.3 0.4 fusion.26
  105.8 3.5 %fusion.44 = (f32[2,512]{1,0:T(2,128)S(1)}, f32[2,512,512]{1,2,0:T(8,128)}) fusion(pred[512,512]{0,1:T(8,128)(4,1)S(1)} %broadcast_compare_fusion, bf16[512,2,256]{0,2,1:T(8,128)(2,1)} %bitcast.82, bf16[64,2,8,256]{3,2,1,0:T(8,128)(2,1)} %bitcast.85), kind=kOutput, calls=%fused_computation.46 | convolution fusion | flops 270533120 | bytes 3411968 | tf_op jit(solution)/shard_map/sub | solution.py:14
  109.2 2.9 %convolution_convert_fusion.1 = bf16[2,512,256]{1,2,0:T(8,128)(2,1)} fusion(bf16[512,2,256]{0,2,1:T(8,128)(2,1)S(1)} %bitcast.79, f32[2,512,512]{1,2,0:T(8,128)} %get-tuple-element.7, f32[2,512]{1,0:T(2,128)S(1)} %get-tuple-element.6), kind=kOutput, calls=%fused_computation.17 | convolution fusion | flops 269746176 | bytes 3149824 | tf_op jit(solution)/shard_map/hqk,qhd->khd/dot_general | solution.py:20
  112.1 4.2 %fusion.13 = bf16[2,512,256]{1,2,0:T(8,128)(2,1)} fusion(bf16[512,2,256]{0,2,1:T(8,128)(2,1)} %bitcast.83, f32[2,512,512]{2,1,0:T(8,128)S(1)} %fusion.26, f32[2,512,512]{1,2,0:T(8,128)} %get-tuple-element.7, f32[2,512]{1,0:T(2,128)S(1)} %get-tuple-element.6), kind=kOutput, calls=%fused_computation.16 | convolution fusion | flops 272369152 | bytes 5246976 | tf_op jit(solution)/shard_map/hqk,qhd->khd/dot_general | solution.py:26
  116.3 10.4 %fusion.2 = bf16[4096,512]{0,1:T(8,128)(2,1)} fusion(bf16[4096,1024]{1,0:T(8,128)(2,1)} %bitcast.77, bf16[512,512]{0,1:T(8,128)(2,1)S(1)} %bitcast.88, bf16[512,512]{0,1:T(8,128)(2,1)} %bitcast.89), kind=kOutput, calls=%fused_computation.3 | convolution fusion | flops 4299161600 | bytes 13631488 | tf_op jit(solution)/shard_map/dot_general | solution.py:58
  126.7 0.0 reduce-scatter.3.cloned.1.call-update
  126.7 0.0 reduce-scatter.5.cloned.1.call-start
  126.8 62.2 %reduce-scatter.3.cloned.1.call-done = bf16[256,512]{0,1:T(8,128)(2,1)} async-done(((bf16[4096,512]{0,1:T(8,128)(2,1)}), bf16[256,512]{0,1:T(8,128)(2,1)}) %reduce-scatter.3.cloned.1.call-update) | async-done | bytes 262160 | tf_op jit(solution)/shard_map/reduce_scatter | solution.py:57
  189.0 0.0 reduce-scatter.5.cloned.1.call-update
  189.0 0.5 convolution_convert_fusion.2
  189.5 1.0 copy.19
  190.5 75.5 %reduce-scatter.5.cloned.1.call-done = bf16[256,64]{0,1:T(8,128)(2,1)} async-done(((bf16[256,512]{0,1:T(8,128)(2,1)}), bf16[256,64]{0,1:T(8,128)(2,1)}) %reduce-scatter.5.cloned.1.call-update) | async-done | bytes 32784 | tf_op jit(solution)/shard_map/reduce_scatter | solution.py:66
  266.0 1.4 convert_bitcast_fusion
  (8 shorter events, 0.0 us)
Async XLA Ops:
  7.2 88.1 %all-gather.4.cloned.1.call-start = ((), (), s32[]{:S(2)}) async-start(), calls=%async_computation.4 | async-start | bytes 4456448 | tf_op jit(solution)/shard_map/all_gather | solution.py:40
  43.5 145.5 %reduce-scatter.3.cloned.1.call-start = ((), (), s32[]{:S(2)}) async-start(), calls=%async_computation.2 | async-start | bytes 4456448 | tf_op jit(solution)/shard_map/reduce_scatter | solution.py:57
  46.9 9.5 %copy-start = (s32[1,512]{1,0:T(1,128)S(1)}, s32[1,512]{1,0:T(1,128)}, u32[]{:S(2)}) copy-start(s32[1,512]{1,0:T(1,128)} %param.11) | copy-start | bytes 6148
  46.9 9.5 %copy-start.1 = (s32[1,512]{1,0:T(1,128)S(1)}, s32[1,512]{1,0:T(1,128)}, u32[]{:S(2)}) copy-start(s32[1,512]{1,0:T(1,128)} %param.10) | copy-start | bytes 6148
  112.1 4.2 %copy-start.2 = (bf16[2,512,256]{1,2,0:T(8,128)(2,1)S(1)}, bf16[2,512,256]{1,2,0:T(8,128)(2,1)}, u32[]{:S(2)}) copy-start(bf16[2,512,256]{1,2,0:T(8,128)(2,1)} %convolution_convert_fusion.1) | copy-start | bytes 1572868
  126.7 62.3 %copy-start.3 = (f32[2,512,512]{1,2,0:T(8,128)S(1)}, f32[2,512,512]{1,2,0:T(8,128)}, u32[]{:S(2)}) copy-start(f32[2,512,512]{1,2,0:T(8,128)} %get-tuple-element.7) | copy-start | bytes 6291460
  126.7 139.3 %reduce-scatter.5.cloned.1.call-start = ((), (), s32[]{:S(2)}) async-start(), calls=%async_computation.3 | async-start | bytes 294912 | tf_op jit(solution)/shard_map/reduce_scatter | solution.py:66
Sparse Core Ops, SparseCore 0:
  43.6 51.6 all-gather.3
  126.8 62.1 reduce-scatter.2
  192.9 73.1 reduce-scatter.4
where the time goes:
time: 274 us
  waiting for transfers between devices  176 us (64%)
  blocking collectives  36.3 us (13%)
  matrix products  31 us (11%)
  local copies, waits for them, and re-layouts  14.7 us (5%)
  between operations  13.8 us (5%)
    reduce_scatter x1, waiting for transfers between devices, per_device(): lax.psum_scatter(feature_share, 'mp', scatter_dimension=1, tiled=True)  75.5 us
    reduce_scatter x1, waiting for transfers between devices, per_device(): lax.psum_scatter(lax.dot_general(weight_rows, grad_both, (((1,), (1,)), (...  62.2 us
    all_gather x1, waiting for transfers between devices, per_device(): lax.all_gather(all_tokens, 'section', axis=1, tiled=True)  38.7 us
    all_gather x1, blocking collectives, per_device(): all_tokens = lax.all_gather(shard_rows, 'mp', axis=0, tiled=True)  36.3 us
    unnamed x10, local copies, waits for them, and re-layouts  10.5 us
    dot_general x1, matrix products, per_device(): lax.dot_general(weight_rows, grad_both, (((1,), (1,)), ((), ())), preferr...  10.4 us
    dot_general x1, matrix products, per_device(): jnp.dot(lax.all_gather(all_tokens, 'section', axis=1, tiled=True), weight...  9.14 us
  transfers between devices with their start and end apart: 3, of which 3 were waited for; matrix products, arithmetic and copies ran while one was open for 5% of the time, Pallas kernels for 0%

commit v1 on v0

--- a/solution.py
+++ b/solution.py
@@ -34,7 +34,9 @@
     width = kv_weight.shape[3]
     model_width = kv_weight.shape[1]
     flat_weight = kv_weight[0].reshape(model_width, 2 * width)
-    all_tokens = lax.all_gather(shard_rows, "mp", axis=0, tiled=True)
+    all_tokens = jnp.concatenate(
+        lax.all_to_all(jnp.stack([shard_rows] * lax.axis_size("mp")), "mp", 0, 0), axis=0
+    )
     weight_rows = flat_weight
     key_values = jnp.dot(
         lax.all_gather(all_tokens, "section", axis=1, tiled=True),

time: 274 us -> 250 us (0.912)
  blocking collectives: 36.3 us -> 14.4 us
    all_gather x1 -> x0, blocking collectives: 36.3 us -> none  [per_device(): all_tokens = lax.all_gather(shard_rows, 'mp', axis=0, tiled=True)]
    all_to_all x0 -> x1, blocking collectives: none -> 14.4 us  [per_device(): lax.all_to_all(jnp.stack([shard_rows] * lax.axis_size('mp')), 'mp', 0, 0)]
    unnamed x10 -> x12, local copies, waits for them, and re-layouts: 10.5 us -> 10.5 us
where the time goes in v1:
time: 250 us
  waiting for transfers between devices  175 us (70%)
  matrix products  30.9 us (12%)
  local copies, waits for them, and re-layouts  14.5 us (6%)
  blocking collectives  14.4 us (6%)
  between operations  13.8 us (6%)
    reduce_scatter x1, waiting for transfers between devices, per_device(): lax.psum_scatter(feature_share, 'mp', scatter_dimension=1, tiled=True)  75.6 us
    reduce_scatter x1, waiting for transfers between devices, per_device(): lax.psum_scatter(lax.dot_general(weight_rows, grad_both, (((1,), (1,)), (...  62.2 us
    all_gather x1, waiting for transfers between devices, per_device(): lax.all_gather(all_tokens, 'section', axis=1, tiled=True)  36.7 us
    all_to_all x1, blocking collectives, per_device(): lax.all_to_all(jnp.stack([shard_rows] * lax.axis_size('mp')), 'mp', 0, 0)  14.4 us
    unnamed x12, local copies, waits for them, and re-layouts  10.5 us
    dot_general x1, matrix products, per_device(): lax.dot_general(weight_rows, grad_both, (((1,), (1,)), ((), ())), preferr...  10.4 us
    dot_general x1, matrix products, per_device(): jnp.dot(lax.all_gather(all_tokens, 'section', axis=1, tiled=True), weight...  9.14 us
  transfers between devices with their start and end apart: 3, of which 3 were waited for; matrix products, arithmetic and copies ran while one was open for 5% of the time, Pallas kernels for 0%

profile of v1, /device:TPU:2, one launch (start us, length us, event | category | flops | bytes accessed | tf_op | source)
XLA Modules:
  0.0 250.0 jit_solution(13774118292123539973)
XLA Ops:
  7.2 0.0 all-gather.2.cloned.1.call-start
  7.2 0.8 stack.3
  8.0 14.4 %all_to_all.5 = bf16[8,64,256]{2,1,0:T(8,128)(2,1)} all-to-all(bf16[8,64,256]{2,1,0:T(8,128)(2,1)S(1)} %stack.3), channel_id=1, replica_groups=mesh['section'=16,'mp'=8,'dp'=2] {'mp'}, dimensions={0} | all-to-all | bytes 524288 | tf_op jit(solution)/shard_map/all_to_all | solution.py:38
  22.4 0.0 all-gather.2.cloned.1.call-update
  22.5 0.0 reduce-scatter.3.cloned.1.call-start
  22.5 2.1 copy.23
  24.6 0.2 copy.24
  24.8 9.5 %copy.27 = bf16[512,8,2,512]{3,1,2,0:T(8,128)(2,1)} copy(bf16[512,8,2,512]{3,2,1,0:T(2,128)(2,1)} %bitcast.73) | data formatting | bytes 16777216
  34.3 0.2 broadcast_compare_fusion
  34.5 36.7 %all-gather.2.cloned.1.call-done = bf16[512,4096]{1,0:T(8,128)(2,1)} async-done(((bf16[512,256]{1,0:T(8,128)(2,1)}), bf16[512,4096]{1,0:T(8,128)(2,1)}) %all-gather.2.cloned.1.call-update) | async-done | bytes 4194320 | tf_op jit(solution)/shard_map/all_gather | solution.py:42
  71.2 9.1 %convolution_convert_fusion.1 = bf16[512,1024]{1,0:T(8,128)(2,1)S(1)} fusion(bf16[512,4096]{1,0:T(8,128)(2,1)} %all-gather.2.cloned.1.call-done, bf16[4096,1024]{1,0:T(8,128)(2,1)} %bitcast.74), kind=kOutput, calls=%fused_computation.13 | convolution fusion | flops 4295491584 | bytes 13631488 | tf_op jit(solution)/shard_map/dot_general | solution.py:41
  80.4 0.9 fusion.38
  81.2 0.4 fusion.21
  81.7 3.5 %fusion.39 = (f32[2,512]{1,0:T(2,128)S(1)}, f32[2,512,512]{1,2,0:T(8,128)}) fusion(pred[512,512]{0,1:T(8,128)(4,1)S(1)} %broadcast_compare_fusion, bf16[512,2,256]{0,2,1:T(8,128)(2,1)} %bitcast.81, bf16[64,2,8,256]{3,2,1,0:T(8,128)(2,1)} %bitcast.84), kind=kOutput, calls=%fused_computation.44 | convolution fusion | flops 270533120 | bytes 3411968 | tf_op jit(solution)/shard_map/sub | solution.py:14
  85.1 2.9 %convolution_convert_fusion.2 = bf16[2,512,256]{1,2,0:T(8,128)(2,1)} fusion(bf16[512,2,256]{0,2,1:T(8,128)(2,1)S(1)} %bitcast.77, f32[2,512,512]{1,2,0:T(8,128)} %get-tuple-element.7, f32[2,512]{1,0:T(2,128)S(1)} %get-tuple-element.6), kind=kOutput, calls=%fused_computation.15 | convolution fusion | flops 269746176 | bytes 3149824 | tf_op jit(solution)/shard_map/hqk,qhd->khd/dot_general | solution.py:20
  88.0 4.2 %fusion.8 = bf16[2,512,256]{1,2,0:T(8,128)(2,1)} fusion(bf16[512,2,256]{0,2,1:T(8,128)(2,1)} %bitcast.82, f32[2,512,512]{2,1,0:T(8,128)S(1)} %fusion.21, f32[2,512,512]{1,2,0:T(8,128)} %get-tuple-element.7, f32[2,512]{1,0:T(2,128)S(1)} %get-tuple-element.6), kind=kOutput, calls=%fused_computation.14 | convolution fusion | flops 272369152 | bytes 5246976 | tf_op jit(solution)/shard_map/hqk,qhd->khd/dot_general | solution.py:26
  92.2 10.4 %fusion.2 = bf16[4096,512]{0,1:T(8,128)(2,1)} fusion(bf16[4096,1024]{1,0:T(8,128)(2,1)} %bitcast.75, bf16[512,512]{0,1:T(8,128)(2,1)S(1)} %bitcast.88, bf16[512,512]{0,1:T(8,128)(2,1)} %bitcast.89), kind=kOutput, calls=%fused_computation.3 | convolution fusion | flops 4299161600 | bytes 13631488 | tf_op jit(solution)/shard_map/dot_general | solution.py:60
  102.6 0.0 reduce-scatter.3.cloned.1.call-update
  102.6 0.0 reduce-scatter.5.cloned.1.call-start
  102.7 62.2 %reduce-scatter.3.cloned.1.call-done = bf16[256,512]{0,1:T(8,128)(2,1)} async-done(((bf16[4096,512]{0,1:T(8,128)(2,1)}), bf16[256,512]{0,1:T(8,128)(2,1)}) %reduce-scatter.3.cloned.1.call-update) | async-done | bytes 262160 | tf_op jit(solution)/shard_map/reduce_scatter | solution.py:59
  164.9 0.5 convolution_convert_fusion.3
  165.4 1.0 copy.19
  166.4 75.6 %reduce-scatter.5.cloned.1.call-done = bf16[256,64]{0,1:T(8,128)(2,1)} async-done(((bf16[256,512]{0,1:T(8,128)(2,1)}), bf16[256,64]{0,1:T(8,128)(2,1)}) %reduce-scatter.5.cloned.1.call-update) | async-done | bytes 32784 | tf_op jit(solution)/shard_map/reduce_scatter | solution.py:68
  242.0 1.4 convert_bitcast_fusion
  (11 shorter events, 0.0 us)
Async XLA Ops:
  7.2 17.4 %copy-start = (bf16[1,1,512,512]{3,2,1,0:T(8,128)(2,1)S(1)}, bf16[1,1,512,512]{3,2,1,0:T(8,128)(2,1)}, u32[]{:S(2)}) copy-start(bf16[1,1,512,512]{3,2,1,0:T(8,128)(2,1)} %param.9) | copy-start | bytes 1572868
  7.2 64.0 %all-gather.2.cloned.1.call-start = ((), (), s32[]{:S(2)}) async-start(), calls=%async_computation.3 | async-start | bytes 4456448 | tf_op jit(solution)/shard_map/all_gather | solution.py:42
  22.5 142.4 %reduce-scatter.3.cloned.1.call-start = ((), (), s32[]{:S(2)}) async-start(), calls=%async_computation.4 | async-start | bytes 4456448 | tf_op jit(solution)/shard_map/reduce_scatter | solution.py:59
  24.8 9.5 %copy-start.1 = (s32[1,512]{1,0:T(1,128)S(1)}, s32[1,512]{1,0:T(1,128)}, u32[]{:S(2)}) copy-start(s32[1,512]{1,0:T(1,128)} %param.11) | copy-start | bytes 6148
  24.8 9.5 %copy-start.2 = (s32[1,512]{1,0:T(1,128)S(1)}, s32[1,512]{1,0:T(1,128)}, u32[]{:S(2)}) copy-start(s32[1,512]{1,0:T(1,128)} %param.10) | copy-start | bytes 6148
  88.0 4.2 %copy-start.3 = (bf16[2,512,256]{1,2,0:T(8,128)(2,1)S(1)}, bf16[2,512,256]{1,2,0:T(8,128)(2,1)}, u32[]{:S(2)}) copy-start(bf16[2,512,256]{1,2,0:T(8,128)(2,1)} %convolution_convert_fusion.2) | copy-start | bytes 1572868
  102.6 62.3 %copy-start.4 = (f32[2,512,512]{1,2,0:T(8,128)S(1)}, f32[2,512,512]{1,2,0:T(8,128)}, u32[]{:S(2)}) copy-start(f32[2,512,512]{1,2,0:T(8,128)} %get-tuple-element.7) | copy-start | bytes 6291460
  102.6 139.4 %reduce-scatter.5.cloned.1.call-start = ((), (), s32[]{:S(2)}) async-start(), calls=%async_computation.5 | async-start | bytes 294912 | tf_op jit(solution)/shard_map/reduce_scatter | solution.py:68
Sparse Core Ops, SparseCore 0:
  22.6 48.5 all-gather.1
  102.7 62.1 reduce-scatter.2
  168.7 73.2 reduce-scatter.4
